TPU v7x, 128 devices: a whole 4x4x4 slice. The times are simulated.
128 devices in a mesh: row: 8 (over x, core), col: 16 (over y, z).
Axes of the slice: x: 4, y: 4, z: 4, core: 2. Of those that a mesh axis runs over, the one named last changes fastest.
Arguments:
- trail: bfloat16 [16384, 16384], P('row', 'col'), may hold values from -0.046875 to 0.046875
- row_one: bfloat16 [128, 16384], P('row', 'col'), may hold values from -0.5 to 0.5
- row_two: bfloat16 [128, 16384], P('row', 'col'), may hold values from -0.5 to 0.5
- diag_one: float32 [128, 128], replicated, may hold values from -1 to 2, as said below
- diag_two: float32 [128, 128], replicated, may hold values from -1 to 2, as said below
- adj_trail: float32 [16384, 16384], P('row', 'col'), may hold values from -6 to 6
- adj_row_one: float32 [128, 16384], P('row', 'col'), may hold values from -6 to 6
- adj_row_two: float32 [128, 16384], P('row', 'col'), may hold values from -6 to 6
- adj_diag_one: float32 [128, 128], replicated, may hold values from -6 to 6
- adj_diag_two: float32 [128, 128], replicated, may hold values from -6 to 6
Outputs:
- grad_trail: bfloat16 [16384, 16384], P('row', 'col')
- grad_row_one: float32 [128, 16384], P('row', 'col')
- grad_row_two: float32 [128, 16384], P('row', 'col')
- grad_diag_one: float32 [128, 128], replicated
- grad_diag_two: float32 [128, 128], replicated
Inputs may be any that keep to these rules, and one draw needn't show every extreme that they name: `diag_one`: lower triangular with a positive diagonal. `diag_two`: lower triangular with a positive diagonal.
All inputs are finite; a program needn't handle non-finite values.
Results may differ from a plain program's by a relative error of at most 0.014.
Values may be sent and summed in bfloat16 or wider, within the bound.
A program may use at most 128 MiB of HBM per device.

v0:
```python
import jax
import jax.numpy as jnp
from jax import lax
from jax.sharding import PartitionSpec as P

exact_mode = lax.Precision.HIGHEST


def from_root(value, axis, source):
    kept = jnp.where(lax.axis_index(axis) == source, value, 0).astype(value.dtype)
    return lax.psum(kept, axis)


def halved_lower(matrix):
    order = matrix.shape[0]
    keep = jnp.tril(jnp.ones((order, order), matrix.dtype)) - 0.5 * jnp.eye(
        order, dtype=matrix.dtype
    )
    return matrix * keep


def inverse_lower(block):
    ident = jnp.eye(block.shape[0], dtype=block.dtype)
    return lax.linalg.triangular_solve(block, ident, left_side=True, lower=True)


def block_adjoint(block, inverse, seed_adj):
    inner = halved_lower(jnp.dot(block.T, seed_adj, precision=exact_mode))
    middle = jnp.dot(inverse.T, inner, precision=exact_mode)
    return halved_lower(jnp.dot(middle, inverse, precision=exact_mode))


def per_device(
    trail,
    row_one,
    row_two,
    diag_one,
    diag_two,
    adj_trail,
    adj_row_one,
    adj_row_two,
    adj_diag_one,
    adj_diag_two,
):
    panel = diag_one.shape[0]
    width = trail.shape[1]
    band = row_one.shape[0]
    last = width - panel
    col_count = lax.axis_size("col")
    col_here = lax.axis_index("col")
    row_start = lax.axis_index("row") * band
    here_one = col_here == col_count - 2
    here_two = col_here == col_count - 1
    full_one, full_two = (
        lax.all_gather(row_one, "row", axis=0, tiled=True),
        lax.all_gather(row_two, "row", axis=0, tiled=True),
    )

    def own_rows(matrix):
        return lax.dynamic_slice_in_dim(matrix, row_start, band, 0)

    def solve_panel(rows, inverse, root):
        whole = from_root(rows, "col", root)
        return jnp.dot(whole, inverse, precision=exact_mode).astype(jnp.bfloat16)

    def summed_block(partial_value, root):
        rows_sum = lax.psum(partial_value, "row")
        return from_root(rows_sum, "col", root)

    inverse_two = inverse_lower(diag_two)
    solved_two = solve_panel(adj_trail[:, last:], inverse_two, col_count - 1)
    partial_two = jnp.dot(solved_two.T, trail[:, last:], preferred_element_type=jnp.float32)
    seed_two = jnp.tril(adj_diag_two - summed_block(partial_two, col_count - 1))
    grad_diag_two = block_adjoint(diag_two, inverse_two, seed_two)
    mirror_two = own_rows(grad_diag_two + grad_diag_two.T)
    rest_two = jnp.dot(mirror_two, full_two.astype(jnp.float32), precision=exact_mode)
    inverse_one = inverse_lower(diag_one)
    crossed = lax.psum_scatter(
        jnp.dot(solved_two.T, trail, preferred_element_type=jnp.float32).astype(jnp.bfloat16),
        "row",
        scatter_dimension=0,
        tiled=True,
    ).astype(jnp.float32)
    adj_two = adj_row_two - crossed - rest_two
    adj_next = adj_trail - jnp.dot(solved_two, full_two, preferred_element_type=jnp.float32)
    stacked = jnp.concatenate([adj_two[:, last:], adj_next[:, last:]], 0)
    solved_one = solve_panel(stacked, inverse_one, col_count - 2)
    head_rows = solved_one[:band]
    tail_rows = solved_one[band:]
    partial_one = jnp.dot(
        head_rows.T, row_two[:, last:], preferred_element_type=jnp.float32
    ) + jnp.dot(tail_rows.T, trail[:, last:], preferred_element_type=jnp.float32)
    seed_one = jnp.tril(adj_diag_one - summed_block(partial_one, col_count - 2))
    grad_diag_one = block_adjoint(diag_one, inverse_one, seed_one)
    mirror_one = own_rows(grad_diag_one + grad_diag_one.T)
    rest_one = jnp.dot(mirror_one, full_one.astype(jnp.float32), precision=exact_mode)
    head_update = jnp.dot(head_rows, full_one, preferred_element_type=jnp.float32)
    two_left = adj_two - head_update
    trail_left = adj_next - jnp.dot(tail_rows, full_one, preferred_element_type=jnp.float32)
    crossed_one = lax.psum_scatter(
        (
            jnp.dot(head_rows.T, row_two, preferred_element_type=jnp.float32)
            + jnp.dot(tail_rows.T, trail, preferred_element_type=jnp.float32)
        ).astype(jnp.bfloat16),
        "row",
        scatter_dimension=0,
        tiled=True,
    ).astype(jnp.float32)
    one_left = adj_row_one - crossed_one - rest_one
    trail_block = jnp.where(
        here_one,
        tail_rows.astype(jnp.float32),
        jnp.where(here_two, solved_two.astype(jnp.float32), trail_left[:, last:]),
    )
    grad_trail = jnp.concatenate([trail_left[:, :last], trail_block], 1).astype(jnp.bfloat16)
    zero_block = jnp.zeros((band, panel), jnp.float32)
    one_block = jnp.where(here_one | here_two, zero_block, one_left[:, last:])
    grad_row_one = jnp.concatenate([one_left[:, :last], one_block], 1)
    two_block = jnp.where(
        here_one, head_rows.astype(jnp.float32), jnp.where(here_two, zero_block, two_left[:, last:])
    )
    grad_row_two = jnp.concatenate([two_left[:, :last], two_block], 1)
    return (grad_trail, grad_row_one, grad_row_two, grad_diag_one, grad_diag_two)


def solution(mesh):
    in_specs = (
        P("row", "col"),
        P("row", "col"),
        P("row", "col"),
        P(),
        P(),
        P("row", "col"),
        P("row", "col"),
        P("row", "col"),
        P(),
        P(),
    )
    out_specs = (P("row", "col"), P("row", "col"), P("row", "col"), P(), P())
    return jax.shard_map(
        per_device, mesh=mesh, in_specs=in_specs, out_specs=out_specs, check_vma=False
    )
```

profile of v0, /device:TPU:0, one launch (start us, length us, event | category | flops | bytes accessed | tf_op | source)
XLA Modules:
  0.0 564.0 jit_solution(18032866646956129577)
XLA Ops:
  7.2 2.3 slice_select_fusion.1
  9.5 0.0 all-reduce.9.cloned.1.call-start
  9.6 0.9 select_bitcast_fusion.1
  10.4 9.8 %custom-call.4 = f32[1,128,128]{1,2,0:T(8,128)S(1)} custom-call(f32[1,128,128]{2,1,0:T(8,128)S(1)} %select_bitcast_fusion.1), custom_call_target="InvertDiagBlocksLowerTriangular" | custom-call | tf_op jit(solution)/shard_map/triangular_solve/custom-call.1 | solution.py:24
  20.3 13.5 %all_gather.6 = bf16[128,1024]{1,0:T(8,128)(2,1)S(1)} all-gather(bf16[16,1024]{1,0:T(8,128)(2,1)} %param.14), channel_id=1, replica_groups=mesh['row'=8,'col'=16] {'row'}, dimensions={0}, use_global_device_ids=true | all-gather | bytes 294912 | tf_op jit(solution)/shard_map/all_gather | solution.py:56
  33.7 0.3 fusion.13
  34.0 67.5 %all-reduce.7.cloned.1.call-done = f32[2048,128]{1,0:T(8,128)} async-done(((f32[2048,128]{1,0:T(8,128)}), f32[2048,128]{1,0:T(8,128)}) %all-reduce.7.cloned.1.call-update) | async-done | bytes 1048592 | tf_op jit(solution)/shard_map/psum | solution.py:11
  101.5 2.2 convolution_convert_fusion.1
  103.7 2.0 fusion.6
  105.8 7.9 %convolution_subtract_fusion.1 = f32[2048,1024]{1,0:T(8,128)} fusion(f32[2048,1024]{1,0:T(8,128)} %param.17, bf16[2048,128]{1,0:T(8,128)(2,1)S(1)} %convolution_convert_fusion.1, bf16[128,1024]{1,0:T(8,128)(2,1)S(1)} %all_gather.6), kind=kOutput, calls=%fused_computation.2 | convolution fusion | flops 538968064 | bytes 17563648 | tf_op jit(solution)/shard_map/dot_general | solution.py:85
  113.6 50.0 %all-reduce.9.cloned.1.call-done = f32[128,128]{1,0:T(8,128)} async-done(((f32[128,128]{1,0:T(8,128)}), f32[128,128]{1,0:T(8,128)}) %all-reduce.9.cloned.1.call-update) | async-done | bytes 65552 | tf_op jit(solution)/shard_map/psum | solution.py:67
  163.6 0.6 broadcast_select_fusion.1
  164.3 0.0 reduce-scatter.7.cloned.1.call-start
  164.3 3.7 convolution_convert_fusion.2
  168.1 79.6 %all-reduce.11.cloned.1.call-done = f32[128,128]{1,0:T(8,128)} async-done(((f32[128,128]{1,0:T(8,128)}), f32[128,128]{1,0:T(8,128)}) %all-reduce.11.cloned.1.call-update) | async-done | bytes 65552 | tf_op jit(solution)/shard_map/psum | solution.py:11
  247.7 1.1 fusion.2
  248.9 0.3 fusion.42
  249.2 0.2 fusion.25
  249.4 0.1 copy.62
  249.5 30.7 %reduce-scatter.7.cloned.1.call-done = bf16[16,1024]{1,0:T(8,128)(2,1)} async-done(((bf16[128,1024]{1,0:T(8,128)(2,1)}), bf16[16,1024]{1,0:T(8,128)(2,1)}) %reduce-scatter.7.cloned.1.call-update) | async-done | bytes 32784 | tf_op jit(solution)/shard_map/reduce_scatter | solution.py:78
  280.2 1.0 convolution_subtract_fusion.4
  281.2 1.0 maximum_select_fusion
  282.4 9.8 %custom-call.5 = f32[1,128,128]{1,2,0:T(8,128)S(1)} custom-call(f32[1,128,128]{2,1,0:T(8,128)S(1)} %select_bitcast_fusion), custom_call_target="InvertDiagBlocksLowerTriangular" | custom-call | tf_op jit(solution)/shard_map/triangular_solve/custom-call.1 | solution.py:24
  292.2 13.0 %all_gather.7 = bf16[128,1024]{1,0:T(8,128)(2,1)S(1)} all-gather(bf16[16,1024]{1,0:T(8,128)(2,1)S(1)} %copy-done.10), channel_id=1, replica_groups=mesh['row'=8,'col'=16] {'row'}, dimensions={0}, use_global_device_ids=true | all-gather | bytes 294912 | tf_op jit(solution)/shard_map/all_gather | solution.py:55
  305.2 0.3 fusion.11
  305.5 64.7 %all-reduce.13.cloned.1.call-done = f32[2064,128]{1,0:T(8,128)} async-done(((f32[2064,128]{1,0:T(8,128)}), f32[2064,128]{1,0:T(8,128)}) %all-reduce.13.cloned.1.call-update) | async-done | bytes 1056784 | tf_op jit(solution)/shard_map/psum | solution.py:11
  370.2 2.2 convolution_convert_fusion
  372.4 0.2 fusion.32
  372.6 0.2 fusion.36
  372.8 0.2 convolution_subtract_fusion.2
  373.0 6.7 %convolution_subtract_fusion = bf16[2048,1024]{1,0:T(8,128)(2,1)} fusion(f32[2048,1024]{1,0:T(8,128)} %convolution_subtract_fusion.1, bf16[128,1024]{1,0:T(8,128)(2,1)S(1)} %all_gather.7, bf16[2064,128]{1,0:T(8,128)(2,1)S(1)} %convolution_convert_fusion), kind=kOutput, calls=%fused_computation.1 | convolution fusion | flops 541065216 | bytes 13369344 | tf_op jit(solution)/shard_map/dot_general | solution.py:99
  379.7 2.0 convolution_add_fusion.1
  381.7 3.6 fusion
  385.4 1.2 fusion.4
  386.7 4.1 slice.97
  390.8 48.5 %all-reduce.15.cloned.1.call-done = f32[128,128]{1,0:T(8,128)} async-done(((f32[128,128]{1,0:T(8,128)}), f32[128,128]{1,0:T(8,128)}) %all-reduce.15.cloned.1.call-update) | async-done | bytes 65552 | tf_op jit(solution)/shard_map/psum | solution.py:67
  439.3 0.6 broadcast_select_fusion
  440.0 0.6 pad_maximum_fusion.2
  440.6 0.0 reduce-scatter.9.cloned.1.call-update
  440.7 4.7 pad_maximum_fusion
  445.4 78.0 %all-reduce.17.cloned.1.call-done = f32[128,128]{1,0:T(8,128)} async-done(((f32[128,128]{1,0:T(8,128)}), f32[128,128]{1,0:T(8,128)}) %all-reduce.17.cloned.1.call-update) | async-done | bytes 65552 | tf_op jit(solution)/shard_map/psum | solution.py:11
  523.4 1.1 fusion.1
  524.6 0.3 fusion.43
  524.8 0.2 fusion.24
  525.1 0.1 copy.67
  525.2 30.3 %reduce-scatter.9.cloned.1.call-done = bf16[16,1024]{1,0:T(8,128)(2,1)} async-done(((bf16[128,1024]{1,0:T(8,128)(2,1)}), bf16[16,1024]{1,0:T(8,128)(2,1)}) %reduce-scatter.9.cloned.1.call-update) | async-done | bytes 32784 | tf_op jit(solution)/shard_map/reduce_scatter | solution.py:100
  555.5 1.0 convolution_subtract_fusion.3
  556.5 0.6 pad_maximum_fusion.1
  (45 shorter events, 0.5 us)
Async XLA Ops:
  7.2 94.3 %all-reduce.7.cloned.1.call-start = ((), (), s32[]{:S(2)}) async-start(), calls=%async_computation.2 | async-start | bytes 2097152 | tf_op jit(solution)/shard_map/psum | solution.py:11
  9.5 154.1 %all-reduce.9.cloned.1.call-start = ((), (), s32[]{:S(2)}) async-start(), calls=%async_computation.3 | async-start | bytes 131072 | tf_op jit(solution)/shard_map/psum | solution.py:67
  105.7 142.0 %all-reduce.11.cloned.1.call-start = ((), (), s32[]{:S(2)}) async-start(), calls=%async_computation.4 | async-start | bytes 131072 | tf_op jit(solution)/shard_map/psum | solution.py:11
  113.6 134.1 %copy-start.1 = (f32[128,128]{1,0:T(8,128)S(1)}, f32[128,128]{1,0:T(8,128)}, u32[]{:S(2)}) copy-start(f32[128,128]{1,0:T(8,128)} %param.16) | copy-start | bytes 196612
  113.6 134.1 %copy-start.6 = (f32[128,128]{1,0:T(8,128)S(1)}, f32[128,128]{1,0:T(8,128)}, u32[]{:S(2)}) copy-start(f32[128,128]{1,0:T(8,128)} %param.21) | copy-start | bytes 196612
  113.6 166.6 %copy-start.7 = (f32[16,1024]{1,0:T(8,128)S(1)}, f32[16,1024]{1,0:T(8,128)}, u32[]{:S(2)}) copy-start(f32[16,1024]{1,0:T(8,128)} %param.19) | copy-start | bytes 196612
  164.3 117.0 %slice-start = ((f32[2048,1024]{1,0:T(8,128)}), f32[2048,128]{1,0:T(8,128)S(1)}, s32[]{:S(2)}) async-start(f32[2048,1024]{1,0:T(8,128)} %convolution_subtract_fusion.1), calls=%async_computation.10 | async-start | bytes 2097152 | tf_op jit(solution)/shard_map/slice | solution.py:86
  164.3 116.0 %reduce-scatter.7.cloned.1.call-start = ((), (), s32[]{:S(2)}) async-start(), calls=%async_computation.8 | async-start | bytes 294912 | tf_op jit(solution)/shard_map/reduce_scatter | solution.py:78
  168.0 114.3 %copy-start.2 = (f32[128,128]{1,0:T(8,128)S(1)}, f32[128,128]{1,0:T(8,128)}, u32[]{:S(2)}) copy-start(f32[128,128]{1,0:T(8,128)} %param.15) | copy-start | bytes 196612
  168.0 124.2 %copy-start.10 = (bf16[16,1024]{1,0:T(8,128)(2,1)S(1)}, bf16[16,1024]{1,0:T(8,128)(2,1)}, u32[]{:S(2)}) copy-start(bf16[16,1024]{1,0:T(8,128)(2,1)} %param.13) | copy-start | bytes 98308
  168.0 204.4 %copy-start.3 = (bf16[16,1024]{1,0:T(8,128)(2,1)S(1)}, bf16[16,1024]{1,0:T(8,128)(2,1)}, u32[]{:S(2)}) copy-start(bf16[16,1024]{1,0:T(8,128)(2,1)} %param.14) | copy-start | bytes 98308
  168.1 202.1 %all-reduce.13.cloned.1.call-start = ((), (), s32[]{:S(2)}) async-start(), calls=%async_computation.5 | async-start | bytes 2113536 | tf_op jit(solution)/shard_map/psum | solution.py:11
  249.4 130.3 %copy-start.4 = (f32[128,128]{1,0:T(8,128)}, f32[128,128]{1,0:T(8,128)S(1)}, u32[]{:S(2)}) copy-start(f32[128,128]{1,0:T(8,128)S(1)} %get-tuple-element.16) | copy-start | bytes 196612
  282.3 157.0 %all-reduce.15.cloned.1.call-start = ((), (), s32[]{:S(2)}) async-start(), calls=%async_computation.6 | async-start | bytes 131072 | tf_op jit(solution)/shard_map/psum | solution.py:67
  373.0 13.7 %copy-start = (f32[16,1024]{1,0:T(8,128)}, f32[16,1024]{1,0:T(8,128)S(1)}, u32[]{:S(2)}) copy-start(f32[16,1024]{1,0:T(8,128)S(1)} %convolution_subtract_fusion.2) | copy-start | bytes 196612
  381.7 141.7 %all-reduce.17.cloned.1.call-start = ((), (), s32[]{:S(2)}) async-start(), calls=%async_computation.7 | async-start | bytes 131072 | tf_op jit(solution)/shard_map/psum | solution.py:11
  386.6 53.4 %slice-start.1 = ((f32[16,1024]{1,0:T(8,128)}), f32[16,896]{1,0:T(8,128)S(1)}, s32[]{:S(2)}) async-start(f32[16,1024]{1,0:T(8,128)} %copy-done), calls=%async_computation.11 | async-start | bytes 114688 | tf_op jit(solution)/shard_map/slice | solution.py:122
  440.0 115.5 %reduce-scatter.9.cloned.1.call-start = ((), (), s32[]{:S(2)}) async-start(), calls=%async_computation.9 | async-start | bytes 294912 | tf_op jit(solution)/shard_map/reduce_scatter | solution.py:100
  440.7 82.7 %copy-start.8 = (f32[128,128]{1,0:T(8,128)S(1)}, f32[128,128]{1,0:T(8,128)}, u32[]{:S(2)}) copy-start(f32[128,128]{1,0:T(8,128)} %param.20) | copy-start | bytes 196612
  440.7 114.8 %copy-start.9 = (f32[16,1024]{1,0:T(8,128)S(1)}, f32[16,1024]{1,0:T(8,128)}, u32[]{:S(2)}) copy-start(f32[16,1024]{1,0:T(8,128)} %param.18) | copy-start | bytes 196612
  525.1 32.1 %copy-start.5 = (f32[128,128]{1,0:T(8,128)}, f32[128,128]{1,0:T(8,128)S(1)}, u32[]{:S(2)}) copy-start(f32[128,128]{1,0:T(8,128)S(1)} %get-tuple-element.18) | copy-start | bytes 196612
Sparse Core Ops, SparseCore 0:
  11.8 89.6 all-reduce.6
  105.8 57.6 all-reduce.8
  167.7 79.9 all-reduce.10
  250.5 29.6 reduce-scatter.6
  284.3 85.8 all-reduce.12
  381.8 57.4 all-reduce.14
  443.4 79.9 all-reduce.16
  525.8 29.6 reduce-scatter.8
where the time goes:
time: 565 us; the launch traced here: 564 us
  waiting for transfers between devices  449 us (79%)
  matrix products  36.6 us (6%)
  other arithmetic  32.3 us (6%)
  blocking collectives  26.5 us (5%)
  between operations  14.4 us (3%)
    psum x4, waiting for transfers between devices, from_root(): return lax.psum(kept, axis)  290 us
    psum x2, waiting for transfers between devices, summed_block(): rows_sum = lax.psum(partial_value, 'row')  98.4 us
    reduce_scatter x1, waiting for transfers between devices, per_device(): lax.psum_scatter(jnp.dot(solved_two.T, trail, preferred_element_type=jnp....  30.7 us
    reduce_scatter x1, waiting for transfers between devices, per_device(): lax.psum_scatter((jnp.dot(head_rows.T, row_two, preferred_element_type=jn...  30.3 us
    another operation x2, other arithmetic, inverse_lower(): return lax.linalg.triangular_solve(block, ident, left_side=True, lower=True)  19.6 us
    all_gather x1, blocking collectives, per_device(): lax.all_gather(row_two, 'row', axis=0, tiled=True)  13.5 us
    all_gather x1, blocking collectives, per_device(): lax.all_gather(row_one, 'row', axis=0, tiled=True)  13 us
  transfers between devices with their start and end apart: 8, of which 8 were waited for; matrix products, arithmetic and copies ran while one was open for 9% of the time, Pallas kernels for 0%

commit v1 on v0

--- a/solution.py
+++ b/solution.py
@@ -42,6 +42,39 @@
     adj_diag_one,
     adj_diag_two,
 ):
+
+    def recover_corner_now(row_dim, axis_tag, load):
+        reached = lax.psum(1, axis_name=axis_tag)
+        heard = lax.axis_index(axis_tag)
+        carry_out, mixed_arr, e_next = (reached, heard, load.shape[row_dim])
+        log = [
+            dev * carry_out if hop_no == row_dim else dev for hop_no, dev in enumerate(load.shape)
+        ]
+        all_rows = jnp.zeros(log, load.dtype)
+        s_next = lax.dynamic_update_slice_in_dim(all_rows, load, mixed_arr * e_next, axis=row_dim)
+        spare = p_next = load
+        pp = 1
+        while pp < carry_out // 2 + 1:
+            spare = lax.ppermute(
+                spare,
+                axis_name=axis_tag,
+                perm=[(hop_no, (hop_no + 1) % carry_out) for hop_no in range(carry_out)],
+            )
+            s_next = lax.dynamic_update_slice_in_dim(
+                s_next, spare, (mixed_arr - pp) % carry_out * e_next, axis=row_dim
+            )
+            if 2 * pp < carry_out:
+                p_next = lax.ppermute(
+                    p_next,
+                    axis_name=axis_tag,
+                    perm=[(hop_no, (hop_no - 1) % carry_out) for hop_no in range(carry_out)],
+                )
+                s_next = lax.dynamic_update_slice_in_dim(
+                    s_next, p_next, (mixed_arr + pp) % carry_out * e_next, axis=row_dim
+                )
+            pp += 1
+        return s_next
+
     panel = diag_one.shape[0]
     width = trail.shape[1]
     band = row_one.shape[0]
@@ -52,7 +85,7 @@
     here_one = col_here == col_count - 2
     here_two = col_here == col_count - 1
     full_one, full_two = (
-        lax.all_gather(row_one, "row", axis=0, tiled=True),
+        recover_corner_now(0, "row", row_one),
         lax.all_gather(row_two, "row", axis=0, tiled=True),
     )
 

time: 565 us -> 565 us (level)
  blocking collectives: 26.5 us -> 13 us
  starting transfers between devices: 0.33 us -> 9.38 us
    all_gather x1 -> x0, blocking collectives: 13 us -> none  [per_device(): lax.all_gather(row_one, 'row', axis=0, tiled=True)]
    ppermute x0 -> x7, starting transfers between devices: none -> 8.87 us  [the longest x3 8.83 us: recover_corner_now(): lax.ppermute(p_next, axis_name=axis_tag, perm=[(hop_no, (hop_no - 1) % ca...]
    ppermute x0 -> x7, waiting for transfers between devices: none -> 7.68 us  [the longest x4 7.67 us: recover_corner_now(): lax.ppermute(spare, axis_name=axis_tag, perm=[(hop_no, (hop_no + 1) % car...]
  transfers between devices with their start and end apart: 8 -> 15, of which waited for: 8 -> 11; matrix products, arithmetic and copies ran while one was open for 9% -> 10% of each run, Pallas kernels for 0% -> 0%
where the time goes in v1:
time: 565 us; the launch traced here: 564 us
  waiting for transfers between devices  453 us (80%)
  matrix products  36.6 us (6%)
  other arithmetic  33.2 us (6%)
  between operations  14.6 us (3%)
  blocking collectives  13 us (2%)
  starting transfers between devices  9.38 us (2%)
    psum x4, waiting for transfers between devices, from_root(): return lax.psum(kept, axis)  285 us
    psum x2, waiting for transfers between devices, summed_block(): rows_sum = lax.psum(partial_value, 'row')  98.4 us
    reduce_scatter x1, waiting for transfers between devices, per_device(): lax.psum_scatter(jnp.dot(solved_two.T, trail, preferred_element_type=jnp....  30.7 us
    reduce_scatter x1, waiting for transfers between devices, per_device(): lax.psum_scatter((jnp.dot(head_rows.T, row_two, preferred_element_type=jn...  30.3 us
    another operation x2, other arithmetic, inverse_lower(): return lax.linalg.triangular_solve(block, ident, left_side=True, lower=True)  19.6 us
    all_gather x1, blocking collectives, per_device(): lax.all_gather(row_two, 'row', axis=0, tiled=True)  13 us
  transfers between devices with their start and end apart: 15, of which 11 were waited for; matrix products, arithmetic and copies ran while one was open for 10% of the time, Pallas kernels for 0%

profile of v1, /device:TPU:0, one launch (start us, length us, event | category | flops | bytes accessed | tf_op | source)
XLA Modules:
  0.0 563.9 jit_solution(12214027530895433746)
XLA Ops:
  7.2 2.3 slice_select_fusion.1
  9.6 2.9 collective-permute-start.1
  12.5 0.8 select_bitcast_fusion.1
  13.4 9.8 %custom-call.4 = f32[1,128,128]{1,2,0:T(8,128)S(1)} custom-call(f32[1,128,128]{2,1,0:T(8,128)S(1)} %select_bitcast_fusion.1), custom_call_target="InvertDiagBlocksLowerTriangular" | custom-call | tf_op jit(solution)/shard_map/triangular_solve/custom-call.1 | solution.py:24
  23.2 0.9 select_bitcast_fusion
  24.1 9.8 %custom-call.5 = f32[1,128,128]{1,2,0:T(8,128)S(1)} custom-call(f32[1,128,128]{2,1,0:T(8,128)S(1)} %select_bitcast_fusion), custom_call_target="InvertDiagBlocksLowerTriangular" | custom-call | tf_op jit(solution)/shard_map/triangular_solve/custom-call.1 | solution.py:24
  33.9 13.0 %all_gather.3 = bf16[128,1024]{1,0:T(8,128)(2,1)S(1)} all-gather(bf16[16,1024]{1,0:T(8,128)(2,1)} %param.14), channel_id=1, replica_groups=mesh['row'=8,'col'=16] {'row'}, dimensions={0}, use_global_device_ids=true | all-gather | bytes 294912 | tf_op jit(solution)/shard_map/all_gather | solution.py:89
  46.9 0.3 fusion.13
  47.2 54.3 %all-reduce.7.cloned.1.call-done = f32[2048,128]{1,0:T(8,128)} async-done(((f32[2048,128]{1,0:T(8,128)}), f32[2048,128]{1,0:T(8,128)}) %all-reduce.7.cloned.1.call-update) | async-done | bytes 1048592 | tf_op jit(solution)/shard_map/psum | solution.py:11
  101.5 2.2 convolution_convert_fusion.1
  103.7 2.0 fusion.6
  105.8 7.9 %convolution_subtract_fusion.1 = f32[2048,1024]{1,0:T(8,128)} fusion(f32[2048,1024]{1,0:T(8,128)} %param.17, bf16[2048,128]{1,0:T(8,128)(2,1)S(1)} %convolution_convert_fusion.1, bf16[128,1024]{1,0:T(8,128)(2,1)S(1)} %all_gather.3), kind=kOutput, calls=%fused_computation.2 | convolution fusion | flops 538968064 | bytes 17563648 | tf_op jit(solution)/shard_map/dot_general | solution.py:118
  113.7 49.9 %all-reduce.9.cloned.1.call-done = f32[128,128]{1,0:T(8,128)} async-done(((f32[128,128]{1,0:T(8,128)}), f32[128,128]{1,0:T(8,128)}) %all-reduce.9.cloned.1.call-update) | async-done | bytes 65552 | tf_op jit(solution)/shard_map/psum | solution.py:100
  163.6 0.6 broadcast_select_fusion.1
  164.3 3.7 convolution_convert_fusion.2
  168.1 79.6 %all-reduce.11.cloned.1.call-done = f32[128,128]{1,0:T(8,128)} async-done(((f32[128,128]{1,0:T(8,128)}), f32[128,128]{1,0:T(8,128)}) %all-reduce.11.cloned.1.call-update) | async-done | bytes 65552 | tf_op jit(solution)/shard_map/psum | solution.py:11
  247.7 1.1 fusion.2
  248.9 0.3 fusion.42
  249.2 0.2 fusion.25
  249.5 30.7 %reduce-scatter.7.cloned.1.call-done = bf16[16,1024]{1,0:T(8,128)(2,1)} async-done(((bf16[128,1024]{1,0:T(8,128)(2,1)}), bf16[16,1024]{1,0:T(8,128)(2,1)}) %reduce-scatter.7.cloned.1.call-update) | async-done | bytes 32784 | tf_op jit(solution)/shard_map/reduce_scatter | solution.py:111
  280.2 1.0 convolution_subtract_fusion.4
  281.2 1.0 maximum_select_fusion
  282.3 0.2 all-reduce.15.cloned.1.call-start
  282.5 0.3 fusion.11
  283.0 2.9 collective-permute-start.3
  286.0 1.6 collective-permute-done.2
  287.6 3.0 collective-permute-start.5
  290.5 1.6 collective-permute-done.4
  292.2 4.5 collective-permute-done.6
  296.7 73.5 %all-reduce.13.cloned.1.call-done = f32[2064,128]{1,0:T(8,128)} async-done(((f32[2064,128]{1,0:T(8,128)}), f32[2064,128]{1,0:T(8,128)}) %all-reduce.13.cloned.1.call-update) | async-done | bytes 1056784 | tf_op jit(solution)/shard_map/psum | solution.py:11
  370.2 2.2 convolution_convert_fusion
  372.6 0.2 fusion.38
  373.0 6.7 %convolution_subtract_fusion = bf16[2048,1024]{1,0:T(8,128)(2,1)} fusion(f32[2048,1024]{1,0:T(8,128)} %convolution_subtract_fusion.1, bf16[128,1024]{1,0:T(8,128)(2,1)S(1)} %constant_dynamic-update-slice_fusion, bf16[2064,128]{1,0:T(8,128)(2,1)S(1)} %convolution_convert_fusion), kind=kOutput, calls=%fused_computation.1 | convolution fusion | flops 541065216 | bytes 13369344 | tf_op jit(solution)/shard_map/dot_general | solution.py:132
  379.6 2.0 convolution_add_fusion.1
  381.7 3.6 fusion
  385.3 1.2 fusion.4
  386.6 4.1 slice.97
  390.8 48.5 %all-reduce.15.cloned.1.call-done = f32[128,128]{1,0:T(8,128)} async-done(((f32[128,128]{1,0:T(8,128)}), f32[128,128]{1,0:T(8,128)}) %all-reduce.15.cloned.1.call-update) | async-done | bytes 65552 | tf_op jit(solution)/shard_map/psum | solution.py:100
  439.3 0.6 broadcast_select_fusion
  440.0 0.6 pad_maximum_fusion.2
  440.7 4.7 pad_maximum_fusion
  445.4 78.0 %all-reduce.17.cloned.1.call-done = f32[128,128]{1,0:T(8,128)} async-done(((f32[128,128]{1,0:T(8,128)}), f32[128,128]{1,0:T(8,128)}) %all-reduce.17.cloned.1.call-update) | async-done | bytes 65552 | tf_op jit(solution)/shard_map/psum | solution.py:11
  523.4 1.1 fusion.1
  524.5 0.3 fusion.43
  524.8 0.2 fusion.24
  525.1 30.3 %reduce-scatter.9.cloned.1.call-done = bf16[16,1024]{1,0:T(8,128)(2,1)} async-done(((bf16[128,1024]{1,0:T(8,128)(2,1)}), bf16[16,1024]{1,0:T(8,128)(2,1)}) %reduce-scatter.9.cloned.1.call-update) | async-done | bytes 32784 | tf_op jit(solution)/shard_map/reduce_scatter | solution.py:133
  555.5 1.0 convolution_subtract_fusion.3
  556.5 0.6 pad_maximum_fusion.1
  (67 shorter events, 1.2 us)
Async XLA Ops:
  7.2 94.3 %all-reduce.7.cloned.1.call-start = ((), (), s32[]{:S(2)}) async-start(), calls=%async_computation.2 | async-start | bytes 2097152 | tf_op jit(solution)/shard_map/psum | solution.py:11
  9.5 154.1 %all-reduce.9.cloned.1.call-start = ((), (), s32[]{:S(2)}) async-start(), calls=%async_computation.3 | async-start | bytes 131072 | tf_op jit(solution)/shard_map/psum | solution.py:100
  9.6 273.4 %collective-permute-start = (bf16[16,1024]{1,0:T(8,128)(2,1)}, bf16[16,1024]{1,0:T(8,128)(2,1)S(1)}, u32[]{:S(2)}, u32[]{:S(2)}) collective-permute-start(bf16[16,1024]{1,0:T(8,128)(2,1)} %param.13), channel_id=1, source_target_pairs={{0,16},{16,32},{32,48},{48,64},{64,80},{80,96},{96,112},{112,0},{1... | collective-permute-start | bytes 98312 | tf_op jit(solution)/shard_map/ppermute | solution.py:58
  9.6 273.4 %collective-permute-start.1 = (bf16[16,1024]{1,0:T(8,128)(2,1)}, bf16[16,1024]{1,0:T(8,128)(2,1)S(1)}, u32[]{:S(2)}, u32[]{:S(2)}) collective-permute-start(bf16[16,1024]{1,0:T(8,128)(2,1)} %param.13), channel_id=1, source_target_pairs={{0,112},{16,0},{32,16},{48,32},{64,48},{80,64},{96,80},{112,96},{1... | collective-permute-start | bytes 98312 | tf_op jit(solution)/shard_map/ppermute | solution.py:67
  105.7 142.0 %all-reduce.11.cloned.1.call-start = ((), (), s32[]{:S(2)}) async-start(), calls=%async_computation.4 | async-start | bytes 131072 | tf_op jit(solution)/shard_map/psum | solution.py:11
  113.7 134.1 %copy-start.1 = (f32[128,128]{1,0:T(8,128)S(1)}, f32[128,128]{1,0:T(8,128)}, u32[]{:S(2)}) copy-start(f32[128,128]{1,0:T(8,128)} %param.16) | copy-start | bytes 196612
  113.7 134.1 %copy-start.6 = (f32[128,128]{1,0:T(8,128)S(1)}, f32[128,128]{1,0:T(8,128)}, u32[]{:S(2)}) copy-start(f32[128,128]{1,0:T(8,128)} %param.21) | copy-start | bytes 196612
  113.7 166.6 %copy-start.7 = (f32[16,1024]{1,0:T(8,128)S(1)}, f32[16,1024]{1,0:T(8,128)}, u32[]{:S(2)}) copy-start(f32[16,1024]{1,0:T(8,128)} %param.19) | copy-start | bytes 196612
  164.3 117.0 %slice-start = ((f32[2048,1024]{1,0:T(8,128)}), f32[2048,128]{1,0:T(8,128)S(1)}, s32[]{:S(2)}) async-start(f32[2048,1024]{1,0:T(8,128)} %convolution_subtract_fusion.1), calls=%async_computation.10 | async-start | bytes 2097152 | tf_op jit(solution)/shard_map/slice | solution.py:119
  164.3 116.0 %reduce-scatter.7.cloned.1.call-start = ((), (), s32[]{:S(2)}) async-start(), calls=%async_computation.8 | async-start | bytes 294912 | tf_op jit(solution)/shard_map/reduce_scatter | solution.py:111
  168.0 114.8 %copy-start.10 = (bf16[16,1024]{1,0:T(8,128)(2,1)S(1)}, bf16[16,1024]{1,0:T(8,128)(2,1)}, u32[]{:S(2)}) copy-start(bf16[16,1024]{1,0:T(8,128)(2,1)} %param.13) | copy-start | bytes 98308
  168.0 204.3 %copy-start.3 = (bf16[16,1024]{1,0:T(8,128)(2,1)S(1)}, bf16[16,1024]{1,0:T(8,128)(2,1)}, u32[]{:S(2)}) copy-start(bf16[16,1024]{1,0:T(8,128)(2,1)} %param.14) | copy-start | bytes 98308
  168.1 202.1 %all-reduce.13.cloned.1.call-start = ((), (), s32[]{:S(2)}) async-start(), calls=%async_computation.5 | async-start | bytes 2113536 | tf_op jit(solution)/shard_map/psum | solution.py:11
  249.4 130.3 %copy-start.4 = (f32[128,128]{1,0:T(8,128)}, f32[128,128]{1,0:T(8,128)S(1)}, u32[]{:S(2)}) copy-start(f32[128,128]{1,0:T(8,128)S(1)} %get-tuple-element.16) | copy-start | bytes 196612
  282.3 157.0 %all-reduce.15.cloned.1.call-start = ((), (), s32[]{:S(2)}) async-start(), calls=%async_computation.6 | async-start | bytes 131072 | tf_op jit(solution)/shard_map/psum | solution.py:100
  283.0 4.6 collective-permute-start.2
  283.0 4.5 collective-permute-start.3
  287.6 4.6 collective-permute-start.4
  287.6 4.6 collective-permute-start.5
  292.1 4.6 collective-permute-start.6
  373.0 13.6 %copy-start = (f32[16,1024]{1,0:T(8,128)}, f32[16,1024]{1,0:T(8,128)S(1)}, u32[]{:S(2)}) copy-start(f32[16,1024]{1,0:T(8,128)S(1)} %convolution_subtract_fusion.2) | copy-start | bytes 196612
  381.7 141.7 %all-reduce.17.cloned.1.call-start = ((), (), s32[]{:S(2)}) async-start(), calls=%async_computation.7 | async-start | bytes 131072 | tf_op jit(solution)/shard_map/psum | solution.py:11
  386.6 53.4 %slice-start.1 = ((f32[16,1024]{1,0:T(8,128)}), f32[16,896]{1,0:T(8,128)S(1)}, s32[]{:S(2)}) async-start(f32[16,1024]{1,0:T(8,128)} %copy-done), calls=%async_computation.11 | async-start | bytes 114688 | tf_op jit(solution)/shard_map/slice | solution.py:155
  439.9 115.5 %reduce-scatter.9.cloned.1.call-start = ((), (), s32[]{:S(2)}) async-start(), calls=%async_computation.9 | async-start | bytes 294912 | tf_op jit(solution)/shard_map/reduce_scatter | solution.py:133
  440.7 82.7 %copy-start.2 = (f32[128,128]{1,0:T(8,128)S(1)}, f32[128,128]{1,0:T(8,128)}, u32[]{:S(2)}) copy-start(f32[128,128]{1,0:T(8,128)} %param.15) | copy-start | bytes 196612
  440.7 82.7 %copy-start.8 = (f32[128,128]{1,0:T(8,128)S(1)}, f32[128,128]{1,0:T(8,128)}, u32[]{:S(2)}) copy-start(f32[128,128]{1,0:T(8,128)} %param.20) | copy-start | bytes 196612
  440.7 114.8 %copy-start.9 = (f32[16,1024]{1,0:T(8,128)S(1)}, f32[16,1024]{1,0:T(8,128)}, u32[]{:S(2)}) copy-start(f32[16,1024]{1,0:T(8,128)} %param.18) | copy-start | bytes 196612
  525.0 32.1 %copy-start.5 = (f32[128,128]{1,0:T(8,128)}, f32[128,128]{1,0:T(8,128)S(1)}, u32[]{:S(2)}) copy-start(f32[128,128]{1,0:T(8,128)S(1)} %get-tuple-element.18) | copy-start | bytes 196612
Sparse Core Ops, SparseCore 0:
  11.8 89.6 all-reduce.6
  105.8 57.6 all-reduce.8
  167.7 79.9 all-reduce.10
  250.5 29.6 reduce-scatter.6
  284.3 85.7 all-reduce.12
  381.8 57.4 all-reduce.14
  443.4 79.9 all-reduce.16
  525.7 29.6 reduce-scatter.8
